TPU v7x, 256 devices: a whole 4x4x8 slice. The times are simulated.
256 devices in a mesh: ha: 8 (over z_lo, core), wa: 32 (over y, x, z_hi).
Axes of the slice: x: 4, y: 4, z: 8 (z_hi: 2, z_lo: 4; z = z_hi * 4 + z_lo), core: 2. Of those that a mesh axis runs over, the one named last changes fastest.
Arguments:
- tokens: bfloat16 [1, 8, 64, 64, 1152], P(None, None, 'ha', 'wa'), may hold values from -36 to 36
- cotangent: bfloat16 [1, 8, 64, 64, 1152], P(None, None, 'ha', 'wa'), may hold values from -6 to 6
- w_qkv: bfloat16 [3, 1152, 1728], P(None, 'wa'), may hold values from -0.1875 to 0.1875
- w_out: bfloat16 [3, 576, 1152], P(None, 'wa'), may hold values from -0.25 to 0.25
- gains: float32 [3, 1152], replicated, may hold values from 0.1 to 1.9
- gates: float32 [3, 8], replicated, may hold values from 0.5 to 2
Outputs:
- token_grad: bfloat16 [1, 8, 64, 64, 1152], P(None, None, 'ha', 'wa')
- head_sens: bfloat16 [1, 3, 8, 64, 64, 8], P(None, None, None, 'ha', 'wa')
All inputs are finite; a program needn't handle non-finite values.
Results may differ from a plain program's by a relative error of at most 0.02.
Values may be sent and summed in bfloat16 or wider, within the bound.
A program may use at most 128 MiB of HBM per device.

v0:
```python
import jax
import jax.numpy as jnp
from jax import lax
from jax.sharding import PartitionSpec as P


def letter_forms(attend_axis):
    letters = "bfhw"
    query_side = letters + "nc"
    key_side = letters[:attend_axis] + "g" + letters[attend_axis + 1 :] + "nc"
    score_side = (
        letters[:attend_axis] + letters[attend_axis + 1 :] + "n" + letters[attend_axis] + "g"
    )
    return (
        query_side + "," + key_side + "->" + score_side,
        score_side + "," + key_side + "->" + query_side,
        score_side + "," + query_side + "->" + key_side,
    )


def product(form, left, right):
    return jnp.einsum(form, left, right, preferred_element_type=jnp.float32)


def forward_sublayer(inputs, w_qkv, w_out, gain, gate, attend_axis, keep_output):
    scores_form, mixing_form, keyward_form = letter_forms(attend_axis)
    heads = gate.shape[0]
    hidden = w_out.shape[0]
    head_dim = hidden // heads
    leading = inputs.shape[:4]
    inputs_f = inputs.astype(jnp.float32)
    inverse = lax.rsqrt(jnp.mean(inputs_f * inputs_f, axis=-1, keepdims=True) + 1e-06)
    normed = (inputs_f * inverse * gain).astype(jnp.bfloat16)
    projected = jnp.dot(normed, w_qkv, preferred_element_type=jnp.float32).astype(jnp.bfloat16)
    split = projected.reshape(leading + (3, heads, head_dim))
    queries = split[..., 0, :, :]
    keys_all = split[..., 1, :, :]
    values = split[..., 2, :, :]
    scores = product(scores_form, queries, keys_all) * head_dim ** (-0.5)
    raised = jnp.exp(scores)
    probs = raised / jnp.sum(raised, axis=-1, keepdims=True)
    probs_half = probs.astype(jnp.bfloat16)
    attended = product(mixing_form, probs_half, values).astype(jnp.bfloat16)
    saved = (inverse, queries, keys_all, values, probs, probs_half, attended)
    if not keep_output:
        return (inputs, saved)
    gated = (
        (attended.astype(jnp.float32) * gate[:, None])
        .astype(jnp.bfloat16)
        .reshape(leading + (hidden,))
    )
    outputs = (inputs_f + jnp.dot(gated, w_out, preferred_element_type=jnp.float32)).astype(
        jnp.bfloat16
    )
    return (outputs, saved)


def backward_sublayer(outgrad, inputs, saved, w_qkv, w_out, gain, gate, attend_axis):
    scores_form, mixing_form, keyward_form = letter_forms(attend_axis)
    inverse, queries, keys_all, values, probs, probs_half, attended = saved
    heads = gate.shape[0]
    hidden = w_out.shape[0]
    head_dim = hidden // heads
    leading = inputs.shape[:4]
    d_gated = jnp.dot(outgrad, w_out.T, preferred_element_type=jnp.float32).astype(jnp.bfloat16)
    d_gated = d_gated.reshape(leading + (heads, head_dim))
    sens = jnp.sum(d_gated.astype(jnp.float32) * attended.astype(jnp.float32), axis=-1).astype(
        jnp.bfloat16
    )
    d_attended = (d_gated.astype(jnp.float32) * gate[:, None]).astype(jnp.bfloat16)
    d_probs = product(scores_form, d_attended, values)
    d_values = product(keyward_form, probs_half, d_attended)
    d_scores = (
        probs * (d_probs - jnp.sum(d_probs * probs, axis=-1, keepdims=True)) * head_dim ** (-0.5)
    ).astype(jnp.bfloat16)
    d_queries = product(mixing_form, d_scores, keys_all)
    d_keys = product(keyward_form, d_scores, queries)
    d_proj = (
        jnp.stack([d_queries, d_keys, d_values], axis=4)
        .reshape(leading + (3 * hidden,))
        .astype(jnp.bfloat16)
    )
    d_normed = jnp.dot(d_proj, w_qkv.T, preferred_element_type=jnp.float32) * gain
    inputs_f = inputs.astype(jnp.float32)
    ingrad = (
        outgrad.astype(jnp.float32)
        + inverse * d_normed
        - inputs_f
        * inverse
        * inverse
        * inverse
        * jnp.mean(inputs_f * d_normed, axis=-1, keepdims=True)
    )
    return (ingrad.astype(jnp.bfloat16), sens)


def per_device(tokens, cotangent, w_qkv, w_out, gains, gates):
    heads = gates.shape[1]

    def weights_for(sublayer):
        return (
            lax.all_gather(w_qkv[sublayer], "wa", axis=0, tiled=True),
            lax.all_gather(w_out[sublayer], "wa", axis=0, tiled=True),
        )

    qkv_first, out_first = weights_for(0)
    after_time, saved_time = forward_sublayer(
        tokens, qkv_first, out_first, gains[0], gates[0], 1, True
    )
    qkv_second, out_second = weights_for(1)
    tall_input = lax.all_to_all(after_time, "ha", split_axis=1, concat_axis=2, tiled=True)
    after_height, saved_height = forward_sublayer(
        tall_input, qkv_second, out_second, gains[1], gates[1], 2, True
    )
    qkv_third, out_third = weights_for(2)
    wide_input = lax.all_to_all(after_height, "wa", split_axis=2, concat_axis=3, tiled=True)
    wide_same, saved_width = forward_sublayer(
        wide_input, qkv_third, out_third, gains[2], gates[2], 3, False
    )
    tall_cot = lax.all_to_all(cotangent, "ha", split_axis=1, concat_axis=2, tiled=True)
    wide_cot = lax.all_to_all(tall_cot, "wa", split_axis=2, concat_axis=3, tiled=True)
    grad_width, sens_width = backward_sublayer(
        wide_cot, wide_input, saved_width, qkv_third, out_third, gains[2], gates[2], 3
    )
    tall_grad, tall_sens = (
        lax.all_to_all(grad_width, "wa", split_axis=3, concat_axis=2, tiled=True),
        lax.all_to_all(sens_width, "wa", split_axis=3, concat_axis=2, tiled=True),
    )
    grad_height, sens_height = backward_sublayer(
        tall_grad, tall_input, saved_height, qkv_second, out_second, gains[1], gates[1], 2
    )
    home_cot, both_sens = (
        lax.all_to_all(grad_height, "ha", split_axis=2, concat_axis=1, tiled=True),
        lax.all_to_all(
            jnp.concatenate([tall_sens, sens_height], axis=-1),
            "ha",
            split_axis=2,
            concat_axis=1,
            tiled=True,
        ),
    )
    home_sens_width = both_sens[..., :heads]
    home_sens_height = both_sens[..., heads:]
    token_grad, sens_time = backward_sublayer(
        home_cot, tokens, saved_time, qkv_first, out_first, gains[0], gates[0], 1
    )
    head_sens = jnp.stack([sens_time, home_sens_height, home_sens_width], axis=1)
    return (token_grad, head_sens)


def solution(mesh):
    in_specs = (
        P(None, None, "ha", "wa", None),
        P(None, None, "ha", "wa", None),
        P(None, "wa", None),
        P(None, "wa", None),
        P(),
        P(),
    )
    out_specs = (P(None, None, "ha", "wa", None), P(None, None, None, "ha", "wa", None))
    return jax.shard_map(
        per_device, mesh=mesh, in_specs=in_specs, out_specs=out_specs, check_vma=False
    )
```

profile of v0, /device:TPU:1, one launch (start us, length us, event | category | flops | bytes accessed | tf_op | source)
XLA Modules:
  0.0 885.5 jit_solution(4877952526610603117)
XLA Ops:
  14.5 7.4 all-to-all-start
  22.7 145.0 %all-gather.13.cloned.1.call-done = bf16[1,1152,1728]{2,0,1:T(2,128)(2,1)} async-done(((bf16[1,36,1728]{2,0,1:T(2,128)(2,1)}), bf16[1,1152,1728]{2,0,1:T(2,128)(2,1)}) %all-gather.13.cloned.1.call-update) | async-done | bytes 3981328 | tf_op jit(solution)/shard_map/all_gather | solution.py:102
  167.7 17.9 %copy.441 = bf16[1,1152,1728]{1,2,0:T(8,128)(2,1)} copy(bf16[1,1152,1728]{2,0,1:T(2,128)(2,1)} %all-gather.13.cloned.1.call-done) | data formatting | bytes 7962624 | tf_op jit(solution)/shard_map/all_gather | solution.py:102
  185.5 3.4 fusion.31
  191.9 66.3 %all-gather.15.cloned.1.call-done = bf16[1,576,1152]{2,0,1:T(2,128)(2,1)} async-done(((bf16[1,18,1152]{2,0,1:T(2,128)(2,1)}), bf16[1,576,1152]{2,0,1:T(2,128)(2,1)}) %all-gather.15.cloned.1.call-update) | async-done | bytes 1327120 | tf_op jit(solution)/shard_map/all_gather | solution.py:103
  261.1 8.8 all-to-all-start.2
  269.9 142.3 %all-gather.17.cloned.1.call-done = bf16[1,1152,1728]{2,0,1:T(2,128)(2,1)} async-done(((bf16[1,36,1728]{2,0,1:T(2,128)(2,1)}), bf16[1,1152,1728]{2,0,1:T(2,128)(2,1)}) %all-gather.17.cloned.1.call-update) | async-done | bytes 3981328 | tf_op jit(solution)/shard_map/all_gather | solution.py:102
  412.3 17.8 %copy.453 = bf16[1,1152,1728]{1,2,0:T(8,128)(2,1)} copy(bf16[1,1152,1728]{2,0,1:T(2,128)(2,1)} %all-gather.17.cloned.1.call-done) | data formatting | bytes 7962624 | tf_op jit(solution)/shard_map/all_gather | solution.py:102
  430.1 5.4 all-to-all-start.1
  435.7 3.4 fusion.25
  442.0 60.2 %all-gather.19.cloned.1.call-done = bf16[1,576,1152]{2,0,1:T(2,128)(2,1)} async-done(((bf16[1,18,1152]{2,0,1:T(2,128)(2,1)}), bf16[1,576,1152]{2,0,1:T(2,128)(2,1)}) %all-gather.19.cloned.1.call-update) | async-done | bytes 1327120 | tf_op jit(solution)/shard_map/all_gather | solution.py:103
  505.4 5.5 all-to-all-start.3
  512.2 84.0 %all-gather.23.cloned.1.call-done = bf16[1,576,1152]{2,0,1:T(2,128)(2,1)} async-done(((bf16[1,18,1152]{2,0,1:T(2,128)(2,1)}), bf16[1,576,1152]{2,0,1:T(2,128)(2,1)}) %all-gather.23.cloned.1.call-update) | async-done | bytes 1327120 | tf_op jit(solution)/shard_map/all_gather | solution.py:103
  599.9 150.2 %all-gather.21.cloned.1.call-done = bf16[1,1152,1728]{2,0,1:T(2,128)(2,1)} async-done(((bf16[1,36,1728]{2,0,1:T(2,128)(2,1)}), bf16[1,1152,1728]{2,0,1:T(2,128)(2,1)}) %all-gather.21.cloned.1.call-update) | async-done | bytes 3981328 | tf_op jit(solution)/shard_map/all_gather | solution.py:102
  750.1 17.8 %copy.465 = bf16[1,1152,1728]{1,2,0:T(8,128)(2,1)} copy(bf16[1,1152,1728]{2,0,1:T(2,128)(2,1)} %all-gather.21.cloned.1.call-done) | data formatting | bytes 7962624 | tf_op jit(solution)/shard_map/all_gather | solution.py:102
  769.0 4.2 fusion.28
  786.8 5.4 all-to-all-start.6
  797.8 5.5 all-to-all-done.6
  803.3 6.1 all-to-all-start.4
  810.3 11.6 %all-to-all-done.4 = bf16[1,1,2,64,1152]{4,2,1,0,3:T(2,128)(2,1)S(1)} async-done(((bf16[1,1,2,64,1152]{4,2,1,0,3:T(2,128)(2,1)}), bf16[1,1,2,64,1152]{4,2,1,0,3:T(2,128)(2,1)S(1)}, u32[]{:S(2)}, u32[]{:S(2)}) %all-to-all-start.4) | async-done | bytes 294944 | tf_op jit(solution)/shard_map/all_to_all | solution.py:126
  822.9 3.1 fusion.85
  836.0 8.8 all-to-all-start.7
  850.4 5.1 all-to-all-start.5
  855.9 8.9 %all-to-all-done.5 = bf16[1,1,64,2,1152]{4,3,1,0,2:T(2,128)(2,1)S(1)} async-done(((bf16[1,1,64,2,1152]{4,3,1,0,2:T(2,128)(2,1)}), bf16[1,1,64,2,1152]{4,3,1,0,2:T(2,128)(2,1)S(1)}, u32[]{:S(2)}, u32[]{:S(2)}) %all-to-all-start.5) | async-done | bytes 294944 | tf_op jit(solution)/shard_map/all_to_all | solution.py:133
  (180 shorter events, 76.3 us)
Async XLA Ops:
  7.2 160.5 %all-gather.13.cloned.1.call-start = ((), (), s32[]{:S(2)}) async-start(), calls=%async_computation.8 | async-start | bytes 8515584 | tf_op jit(solution)/shard_map/all_gather | solution.py:102
  9.3 249.0 %all-gather.15.cloned.1.call-start = ((), (), s32[]{:S(2)}) async-start(), calls=%async_computation.9 | async-start | bytes 2737152 | tf_op jit(solution)/shard_map/all_gather | solution.py:103
  10.9 401.3 %all-gather.17.cloned.1.call-start = ((), (), s32[]{:S(2)}) async-start(), calls=%async_computation.10 | async-start | bytes 8515584 | tf_op jit(solution)/shard_map/all_gather | solution.py:102
  12.0 490.3 %all-gather.19.cloned.1.call-start = ((), (), s32[]{:S(2)}) async-start(), calls=%async_computation.11 | async-start | bytes 2737152 | tf_op jit(solution)/shard_map/all_gather | solution.py:103
  12.7 583.5 %all-gather.23.cloned.1.call-start = ((), (), s32[]{:S(2)}) async-start(), calls=%async_computation.13 | async-start | bytes 2737152 | tf_op jit(solution)/shard_map/all_gather | solution.py:103
  13.5 736.6 %all-gather.21.cloned.1.call-start = ((), (), s32[]{:S(2)}) async-start(), calls=%async_computation.12 | async-start | bytes 8515584 | tf_op jit(solution)/shard_map/all_gather | solution.py:102
  14.5 246.7 %all-to-all-start = ((bf16[1,8,8,2,1152]{4,3,2,0,1:T(2,128)(2,1)}), bf16[1,8,8,2,1152]{4,3,2,0,1:T(2,128)(2,1)}, u32[]{:S(2)}, u32[]{:S(2)}) async-start(bf16[1,8,8,2,1152]{4,3,2,0,1:T(2,128)(2,1)} %bitcast.371), calls=%async_computation | async-start | bytes 589824 | tf_op jit(solution)/shard_map/all_to_all | solution.py:120
  21.9 163.6 %copy-start.19 = (f32[1152]{0:T(1024)}, f32[1152]{0:T(1024)S(1)}, u32[]{:S(2)}) copy-start(f32[1152]{0:T(1024)S(1)} %get-tuple-element.21) | copy-start | bytes 13828
  22.6 167.9 %copy-start.26 = (f32[8]{0:T(128)}, f32[8]{0:T(128)S(1)}, u32[]{:S(2)}) copy-start(f32[8]{0:T(128)S(1)} %get-tuple-element.41) | copy-start | bytes 100
  22.6 162.9 %copy-start.17 = (f32[8,8,2]{1,2,0:T(2,128)}, f32[8,8,2]{1,2,0:T(2,128)S(1)}, u32[]{:S(2)}) copy-start(f32[8,8,2]{1,2,0:T(2,128)S(1)} %add_rsqrt_fusion.2) | copy-start | bytes 1540
  190.0 71.1 %copy-start.14 = (bf16[1,8,8,2,1,8,72]{6,5,4,2,3,1,0:T(8,128)(2,1)}, bf16[1,8,8,2,1,8,72]{6,5,4,2,3,1,0:T(8,128)(2,1)S(1)}, u32[]{:S(2)}) copy-start(bf16[1,8,8,2,1,8,72]{6,5,4,2,3,1,0:T(8,128)(2,1)S(1)} %get-tuple-element.31) | copy-start | bytes 442372
  261.1 168.9 %all-to-all-start.2 = ((bf16[1,8,8,2,1152]{4,2,3,0,1:T(8,128)(2,1)}), bf16[1,8,8,2,1152]{4,2,3,0,1:T(8,128)(2,1)S(1)}, u32[]{:S(2)}, u32[]{:S(2)}) async-start(bf16[1,8,8,2,1152]{4,2,3,0,1:T(8,128)(2,1)} %fusion.37), calls=%async_computation.2 | async-start | bytes 589824 | tf_op jit(solution)/shard_map/all_to_all | solution.py:111
  430.1 75.3 %all-to-all-start.1 = ((bf16[1,1,64,2,1152]{4,3,1,0,2:T(2,128)(2,1)}), bf16[1,1,64,2,1152]{4,3,1,0,2:T(2,128)(2,1)}, u32[]{:S(2)}, u32[]{:S(2)}) async-start(bf16[1,1,64,2,1152]{4,3,1,0,2:T(2,128)(2,1)} %bitcast.2), calls=%async_computation.1 | async-start | bytes 589824 | tf_op jit(solution)/shard_map/all_to_all | solution.py:121
  440.2 65.3 %copy-start.1 = (bf16[1,1,64,2,1,8,72]{6,5,4,2,3,1,0:T(8,128)(2,1)}, bf16[1,1,64,2,1,8,72]{6,5,4,2,3,1,0:T(8,128)(2,1)S(1)}, u32[]{:S(2)}) copy-start(bf16[1,1,64,2,1,8,72]{6,5,4,2,3,1,0:T(8,128)(2,1)S(1)} %get-tuple-element.26) | copy-start | bytes 442372
  440.2 65.3 %copy-start.15 = (bf16[1,1,64,2,1,8,72]{6,5,4,2,3,1,0:T(8,128)(2,1)}, bf16[1,1,64,2,1,8,72]{6,5,4,2,3,1,0:T(8,128)(2,1)S(1)}, u32[]{:S(2)}) copy-start(bf16[1,1,64,2,1,8,72]{6,5,4,2,3,1,0:T(8,128)(2,1)S(1)} %get-tuple-element.27) | copy-start | bytes 442372
  440.2 65.3 %copy-start.16 = (bf16[1,1,64,2,1,8,72]{6,5,4,2,3,1,0:T(8,128)(2,1)}, bf16[1,1,64,2,1,8,72]{6,5,4,2,3,1,0:T(8,128)(2,1)S(1)}, u32[]{:S(2)}) copy-start(bf16[1,1,64,2,1,8,72]{6,5,4,2,3,1,0:T(8,128)(2,1)S(1)} %get-tuple-element.28) | copy-start | bytes 442372
  440.5 64.9 %copy-start.3 = (f32[2,8,64,64]{2,3,1,0:T(8,128)}, f32[2,8,64,64]{2,3,1,0:T(8,128)S(1)}, u32[]{:S(2)}) copy-start(f32[2,8,64,64]{2,3,1,0:T(8,128)S(1)} %fusion.155) | copy-start | bytes 786436
  505.4 262.4 %all-to-all-start.3 = ((bf16[1,1,64,2,1152]{4,3,1,0,2:T(2,128)(2,1)}), bf16[1,1,64,2,1152]{4,3,1,0,2:T(2,128)(2,1)S(1)}, u32[]{:S(2)}, u32[]{:S(2)}) async-start(bf16[1,1,64,2,1152]{4,3,1,0,2:T(2,128)(2,1)} %copy.460), calls=%async_computation.3 | async-start | bytes 589824 | tf_op jit(solution)/shard_map/all_to_all | solution.py:116
  512.2 255.7 %copy-start.7 = (bf16[2,64,1152]{2,1,0:T(8,128)(2,1)}, bf16[2,64,1152]{2,1,0:T(8,128)(2,1)S(1)}, u32[]{:S(2)}) copy-start(bf16[2,64,1152]{2,1,0:T(8,128)(2,1)S(1)} %all_to_all.85) | copy-start | bytes 884740
  786.8 16.5 %all-to-all-start.6 = ((bf16[1,1,2,64,8]{4,2,1,0,3:T(2,128)(2,1)}), bf16[1,1,2,64,8]{4,2,1,0,3:T(2,128)(2,1)}, u32[]{:S(2)}, u32[]{:S(2)}) async-start(bf16[1,1,2,64,8]{4,2,1,0,3:T(2,128)(2,1)} %copy.488), calls=%async_computation.6 | async-start | bytes 65536 | tf_op jit(solution)/shard_map/all_to_all | solution.py:127
  796.8 33.7 %copy-start.4 = (f32[2,8,64,64]{2,3,1,0:T(8,128)S(1)}, f32[2,8,64,64]{2,3,1,0:T(8,128)}, u32[]{:S(2)}) copy-start(f32[2,8,64,64]{2,3,1,0:T(8,128)} %copy-done.3) | copy-start | bytes 786436
  803.3 18.6 %all-to-all-start.4 = ((bf16[1,1,2,64,1152]{4,2,1,0,3:T(2,128)(2,1)}), bf16[1,1,2,64,1152]{4,2,1,0,3:T(2,128)(2,1)S(1)}, u32[]{:S(2)}, u32[]{:S(2)}) async-start(bf16[1,1,2,64,1152]{4,2,1,0,3:T(2,128)(2,1)} %copy.473), calls=%async_computation.4 | async-start | bytes 589824 | tf_op jit(solution)/shard_map/all_to_all | solution.py:126
  836.0 14.4 %all-to-all-start.7 = ((bf16[8,2,128]{2,1,0:T(2,128)(2,1)}), bf16[8,2,128]{2,1,0:T(2,128)(2,1)S(1)}, u32[]{:S(2)}, u32[]{:S(2)}) async-start(bf16[8,2,128]{2,1,0:T(2,128)(2,1)} %reshape.584), calls=%async_computation.7 | async-start | bytes 8192 | tf_op jit(solution)/shard_map/all_to_all | solution.py:134
  850.4 14.4 %all-to-all-start.5 = ((bf16[1,1,64,2,1152]{4,3,1,0,2:T(2,128)(2,1)}), bf16[1,1,64,2,1152]{4,3,1,0,2:T(2,128)(2,1)S(1)}, u32[]{:S(2)}, u32[]{:S(2)}) async-start(bf16[1,1,64,2,1152]{4,3,1,0,2:T(2,128)(2,1)} %copy.478), calls=%async_computation.5 | async-start | bytes 589824 | tf_op jit(solution)/shard_map/all_to_all | solution.py:133
  (21 other events, 177.5 us)
Sparse Core Ops, SparseCore 0:
  12.1 155.5 all-gather.12
  171.6 86.6 all-gather.14
  261.8 150.4 all-gather.16
  415.5 86.6 all-gather.18
  505.5 90.7 all-gather.22
  599.6 150.4 all-gather.20
where the time goes:
time: 888 us; the launch traced here: 885 us
  waiting for transfers between devices  674 us (76%)
  local copies, waits for them, and re-layouts  86.3 us (10%)
  matrix products  53.3 us (6%)
  starting transfers between devices  52.7 us (6%)
  between operations  14.9 us (2%)
    all_gather x3, waiting for transfers between devices, weights_for(): lax.all_gather(w_qkv[sublayer], 'wa', axis=0, tiled=True)  438 us
    all_gather x3, waiting for transfers between devices, weights_for(): lax.all_gather(w_out[sublayer], 'wa', axis=0, tiled=True)  211 us
    all_gather x3, local copies, waits for them, and re-layouts, weights_for(): lax.all_gather(w_qkv[sublayer], 'wa', axis=0, tiled=True)  53.5 us
    dot_general x15, matrix products, product(): return jnp.einsum(form, left, right, preferred_element_type=jnp.float32)  18.4 us
  transfers between devices with their start and end apart: 14, of which 9 were waited for; matrix products, arithmetic and copies ran while one was open for 11% of the time, Pallas kernels for 0%

commit v1 on v0

--- a/solution.py
+++ b/solution.py
@@ -99,7 +99,10 @@
 
     def weights_for(sublayer):
         return (
-            lax.all_gather(w_qkv[sublayer], "wa", axis=0, tiled=True),
+            jnp.concatenate(
+                lax.all_to_all(jnp.stack([w_qkv[sublayer]] * lax.axis_size("wa")), "wa", 0, 0),
+                axis=0,
+            ),
             lax.all_gather(w_out[sublayer], "wa", axis=0, tiled=True),
         )
 

time: 888 us -> 734 us (0.83)
  waiting for transfers between devices: 674 us -> 395 us
  blocking collectives: 0 us -> 144 us
  local copies, waits for them, and re-layouts: 86.3 us -> 57 us
    all_gather x3 -> x0, waiting for transfers between devices: 438 us -> none  [weights_for(): lax.all_gather(w_qkv[sublayer], 'wa', axis=0, tiled=True)]
    all_gather x3, waiting for transfers between devices: 211 us -> 361 us  [weights_for(): lax.all_gather(w_out[sublayer], 'wa', axis=0, tiled=True)]
    all_to_all x0 -> x3, blocking collectives: none -> 144 us  [the longest x1 109 us: weights_for(): lax.all_to_all(jnp.stack([w_qkv[sublayer]] * lax.axis_size('wa')), 'wa',...]
    all_gather x3 -> x0, local copies, waits for them, and re-layouts: 53.5 us -> none  [weights_for(): lax.all_gather(w_qkv[sublayer], 'wa', axis=0, tiled=True)]
    reshape x0 -> x3, local copies, waits for them, and re-layouts: none -> 21.9 us  [weights_for(): jnp.concatenate(lax.all_to_all(jnp.stack([w_qkv[sublayer]] * lax.axis_siz...]
    all_to_all x1, waiting for transfers between devices: 0.01 us -> 11.9 us  [per_device(): lax.all_to_all(tall_cot, 'wa', split_axis=2, concat_axis=3, tiled=True)]
  transfers between devices with their start and end apart: 14 -> 11, of which waited for: 9 -> 7; matrix products, arithmetic and copies ran while one was open for 11% -> 9% of each run, Pallas kernels for 0% -> 0%
where the time goes in v1:
time: 734 us; the launch traced here: 732 us
  waiting for transfers between devices  395 us (54%)
  blocking collectives  144 us (20%)
  starting transfers between devices  58.9 us (8%)
  local copies, waits for them, and re-layouts  57 us (8%)
  matrix products  54 us (7%)
  between operations  14.5 us (2%)
  other arithmetic  8.56 us (1%)
    all_gather x3, waiting for transfers between devices, weights_for(): lax.all_gather(w_out[sublayer], 'wa', axis=0, tiled=True)  361 us
    all_to_all x1, blocking collectives, weights_for(): lax.all_to_all(jnp.stack([w_qkv[sublayer]] * lax.axis_size('wa')), 'wa',...  109 us
    reshape x3, local copies, waits for them, and re-layouts, weights_for(): jnp.concatenate(lax.all_to_all(jnp.stack([w_qkv[sublayer]] * lax.axis_siz...  21.9 us
    dot_general x15, matrix products, product(): return jnp.einsum(form, left, right, preferred_element_type=jnp.float32)  19.7 us
    all_to_all x1, blocking collectives, per_device(): lax.all_to_all(after_time, 'ha', split_axis=1, concat_axis=2, tiled=True)  17.7 us
    all_to_all x1, blocking collectives, per_device(): lax.all_to_all(cotangent, 'ha', split_axis=1, concat_axis=2, tiled=True)  17.3 us
  transfers between devices with their start and end apart: 11, of which 7 were waited for; matrix products, arithmetic and copies ran while one was open for 9% of the time, Pallas kernels for 0%

profile of v1, /device:TPU:1, one launch (start us, length us, event | category | flops | bytes accessed | tf_op | source)
XLA Modules:
  0.0 732.0 jit_solution(14964944528584324870)
XLA Ops:
  7.2 17.3 %all_to_all.123 = bf16[1,8,8,2,1152]{4,3,2,0,1:T(2,128)(2,1)} all-to-all(bf16[1,8,8,2,1152]{4,3,2,0,1:T(2,128)(2,1)} %bitcast.379), channel_id=1, replica_groups=mesh['ha'=8,'wa'=32] {'ha'}, dimensions={1} | all-to-all | bytes 589824 | tf_op jit(solution)/shard_map/all_to_all | solution.py:123
  24.5 11.7 %all-to-all-start.1 = ((bf16[1,1,64,2,1152]{4,3,1,0,2:T(2,128)(2,1)}), bf16[1,1,64,2,1152]{4,3,1,0,2:T(2,128)(2,1)S(1)}, u32[]{:S(2)}, u32[]{:S(2)}) async-start(bf16[1,1,64,2,1152]{4,3,1,0,2:T(2,128)(2,1)} %bitcast.2), calls=%async_computation.1 | async-start | bytes 589824 | tf_op jit(solution)/shard_map/all_to_all | solution.py:124
  37.3 11.9 %all-to-all-done.1 = bf16[1,1,64,2,1152]{4,3,1,0,2:T(2,128)(2,1)S(1)} async-done(((bf16[1,1,64,2,1152]{4,3,1,0,2:T(2,128)(2,1)}), bf16[1,1,64,2,1152]{4,3,1,0,2:T(2,128)(2,1)S(1)}, u32[]{:S(2)}, u32[]{:S(2)}) %all-to-all-start.1) | async-done | bytes 294944 | tf_op jit(solution)/shard_map/all_to_all | solution.py:124
  49.5 108.9 %all_to_all.124 = bf16[32,36,1728]{2,1,0:T(8,128)(2,1)} all-to-all(bf16[32,36,1728]{2,1,0:T(8,128)(2,1)S(1)} %stack.55), channel_id=1, replica_groups=mesh['ha'=8,'wa'=32] {'wa'}, dimensions={0} | all-to-all | bytes 7962624 | tf_op jit(solution)/shard_map/all_to_all | solution.py:103
  160.9 5.5 all-to-all-start.4
  168.7 7.3 reshape.707
  182.1 135.3 %all-gather.7.cloned.1.call-done = bf16[1,576,1152]{2,0,1:T(2,128)(2,1)} async-done(((bf16[1,18,1152]{2,0,1:T(2,128)(2,1)}), bf16[1,576,1152]{2,0,1:T(2,128)(2,1)}) %all-gather.7.cloned.1.call-update) | async-done | bytes 1327120 | tf_op jit(solution)/shard_map/all_gather | solution.py:106
  319.6 17.7 %all_to_all.125 = bf16[1,8,8,2,1152]{4,2,3,0,1:T(8,128)(2,1)S(1)} all-to-all(bf16[1,8,8,2,1152]{4,2,3,0,1:T(8,128)(2,1)S(1)} %fusion.37), channel_id=1, replica_groups=mesh['ha'=8,'wa'=32] {'ha'}, dimensions={1} | all-to-all | bytes 589824 | tf_op jit(solution)/shard_map/all_to_all | solution.py:114
  339.8 5.5 all-to-all-start.6
  346.8 7.3 reshape.713
  360.4 140.2 %all-gather.9.cloned.1.call-done = bf16[1,576,1152]{2,0,1:T(2,128)(2,1)} async-done(((bf16[1,18,1152]{2,0,1:T(2,128)(2,1)}), bf16[1,576,1152]{2,0,1:T(2,128)(2,1)}) %all-gather.9.cloned.1.call-update) | async-done | bytes 1327120 | tf_op jit(solution)/shard_map/all_gather | solution.py:106
  503.8 5.5 all-to-all-start.5
  509.7 85.0 %all-gather.11.cloned.1.call-done = bf16[1,576,1152]{2,0,1:T(2,128)(2,1)} async-done(((bf16[1,18,1152]{2,0,1:T(2,128)(2,1)}), bf16[1,576,1152]{2,0,1:T(2,128)(2,1)}) %all-gather.11.cloned.1.call-update) | async-done | bytes 1327120 | tf_op jit(solution)/shard_map/all_gather | solution.py:106
  598.3 7.3 reshape.719
  623.7 5.3 all-to-all-start.9
  631.2 3.7 multiply_reduce_fusion.3
  640.0 9.0 %all-to-all-start.7 = ((bf16[1,1,2,64,1152]{4,2,1,0,3:T(2,128)(2,1)}), bf16[1,1,2,64,1152]{4,2,1,0,3:T(2,128)(2,1)S(1)}, u32[]{:S(2)}, u32[]{:S(2)}) async-start(bf16[1,1,2,64,1152]{4,2,1,0,3:T(2,128)(2,1)} %copy.445), calls=%async_computation.7 | async-start | bytes 589824 | tf_op jit(solution)/shard_map/all_to_all | solution.py:129
  649.3 12.0 %all-to-all-done.7 = bf16[1,1,2,64,1152]{4,2,1,0,3:T(2,128)(2,1)S(1)} async-done(((bf16[1,1,2,64,1152]{4,2,1,0,3:T(2,128)(2,1)}), bf16[1,1,2,64,1152]{4,2,1,0,3:T(2,128)(2,1)S(1)}, u32[]{:S(2)}, u32[]{:S(2)}) %all-to-all-start.7) | async-done | bytes 294944 | tf_op jit(solution)/shard_map/all_to_all | solution.py:129
  662.3 3.1 fusion.85
  676.9 11.2 %all-to-all-start.10 = ((bf16[8,2,128]{2,1,0:T(2,128)(2,1)}), bf16[8,2,128]{2,1,0:T(2,128)(2,1)S(1)}, u32[]{:S(2)}, u32[]{:S(2)}) async-start(bf16[8,2,128]{2,1,0:T(2,128)(2,1)} %reshape.755), calls=%async_computation.10 | async-start | bytes 8192 | tf_op jit(solution)/shard_map/all_to_all | solution.py:137
  690.4 3.7 fusion.126
  696.3 5.1 all-to-all-start.8
  703.0 7.7 %all-to-all-done.8 = bf16[1,1,64,2,1152]{4,3,1,0,2:T(2,128)(2,1)S(1)} async-done(((bf16[1,1,64,2,1152]{4,3,1,0,2:T(2,128)(2,1)}), bf16[1,1,64,2,1152]{4,3,1,0,2:T(2,128)(2,1)S(1)}, u32[]{:S(2)}, u32[]{:S(2)}) %all-to-all-start.8) | async-done | bytes 294944 | tf_op jit(solution)/shard_map/all_to_all | solution.py:136
  720.4 3.7 fusion.131
  (183 shorter events, 86.5 us)
Async XLA Ops:
  24.5 24.7 %all-to-all-start.1 = ((bf16[1,1,64,2,1152]{4,3,1,0,2:T(2,128)(2,1)}), bf16[1,1,64,2,1152]{4,3,1,0,2:T(2,128)(2,1)S(1)}, u32[]{:S(2)}, u32[]{:S(2)}) async-start(bf16[1,1,64,2,1152]{4,3,1,0,2:T(2,128)(2,1)} %bitcast.2), calls=%async_computation.1 | async-start | bytes 589824 | tf_op jit(solution)/shard_map/all_to_all | solution.py:124
  160.9 158.7 %all-to-all-start.4 = ((bf16[32,36,1728]{2,1,0:T(8,128)(2,1)}), bf16[32,36,1728]{2,1,0:T(8,128)(2,1)}, u32[]{:S(2)}, u32[]{:S(2)}) async-start(bf16[32,36,1728]{2,1,0:T(8,128)(2,1)} %stack.56), calls=%async_computation.4 | async-start | bytes 9175040 | tf_op jit(solution)/shard_map/all_to_all | solution.py:103
  166.4 151.0 %all-gather.7.cloned.1.call-start = ((), (), s32[]{:S(2)}) async-start(), calls=%async_computation.11 | async-start | bytes 2737152 | tf_op jit(solution)/shard_map/all_gather | solution.py:106
  168.7 12.1 %copy-start.26 = (f32[8]{0:T(128)}, f32[8]{0:T(128)S(1)}, u32[]{:S(2)}) copy-start(f32[8]{0:T(128)S(1)} %get-tuple-element.39) | copy-start | bytes 100
  168.7 190.3 %copy-start.28 = (f32[8]{0:T(128)}, f32[8]{0:T(128)S(1)}, u32[]{:S(2)}) copy-start(f32[8]{0:T(128)S(1)} %get-tuple-element.40) | copy-start | bytes 100
  339.8 164.1 %all-to-all-start.6 = ((bf16[32,36,1728]{2,1,0:T(8,128)(2,1)}), bf16[32,36,1728]{2,1,0:T(8,128)(2,1)}, u32[]{:S(2)}, u32[]{:S(2)}) async-start(bf16[32,36,1728]{2,1,0:T(8,128)(2,1)} %stack.57), calls=%async_computation.6 | async-start | bytes 9175040 | tf_op jit(solution)/shard_map/all_to_all | solution.py:103
  345.3 155.4 %all-gather.9.cloned.1.call-start = ((), (), s32[]{:S(2)}) async-start(), calls=%async_computation.12 | async-start | bytes 2737152 | tf_op jit(solution)/shard_map/all_gather | solution.py:106
  346.0 248.6 %all-gather.11.cloned.1.call-start = ((), (), s32[]{:S(2)}) async-start(), calls=%async_computation.13 | async-start | bytes 2737152 | tf_op jit(solution)/shard_map/all_gather | solution.py:106
  358.3 145.6 %copy-start.2 = (bf16[1,1,64,2,1,8,72]{6,5,4,2,3,1,0:T(8,128)(2,1)}, bf16[1,1,64,2,1,8,72]{6,5,4,2,3,1,0:T(8,128)(2,1)S(1)}, u32[]{:S(2)}) copy-start(bf16[1,1,64,2,1,8,72]{6,5,4,2,3,1,0:T(8,128)(2,1)S(1)} %get-tuple-element.24) | copy-start | bytes 442372
  358.3 145.6 %copy-start.17 = (bf16[1,1,64,2,1,8,72]{6,5,4,2,3,1,0:T(8,128)(2,1)}, bf16[1,1,64,2,1,8,72]{6,5,4,2,3,1,0:T(8,128)(2,1)S(1)}, u32[]{:S(2)}) copy-start(bf16[1,1,64,2,1,8,72]{6,5,4,2,3,1,0:T(8,128)(2,1)S(1)} %get-tuple-element.26) | copy-start | bytes 442372
  358.6 238.4 %copy-start.4 = (f32[2,8,64,64]{2,3,1,0:T(8,128)}, f32[2,8,64,64]{2,3,1,0:T(8,128)S(1)}, u32[]{:S(2)}) copy-start(f32[2,8,64,64]{2,3,1,0:T(8,128)S(1)} %fusion.155) | copy-start | bytes 786436
  503.8 101.8 %all-to-all-start.5 = ((bf16[1,1,64,2,1152]{4,3,1,0,2:T(2,128)(2,1)}), bf16[1,1,64,2,1152]{4,3,1,0,2:T(2,128)(2,1)S(1)}, u32[]{:S(2)}, u32[]{:S(2)}) async-start(bf16[1,1,64,2,1152]{4,3,1,0,2:T(2,128)(2,1)} %copy.426), calls=%async_computation.5 | async-start | bytes 589824 | tf_op jit(solution)/shard_map/all_to_all | solution.py:119
  509.7 85.0 %copy-start.9 = (bf16[2,64,1152]{2,1,0:T(8,128)(2,1)}, bf16[2,64,1152]{2,1,0:T(8,128)(2,1)S(1)}, u32[]{:S(2)}) copy-start(bf16[2,64,1152]{2,1,0:T(8,128)(2,1)S(1)} %all_to_all.94) | copy-start | bytes 884740
  616.3 12.7 %copy-start.13 = (bf16[1,1,2,64,1,8,72]{6,3,5,2,4,1,0:T(8,128)(2,1)S(1)}, bf16[1,1,2,64,1,8,72]{6,3,5,2,4,1,0:T(8,128)(2,1)}, u32[]{:S(2)}) copy-start(bf16[1,1,2,64,1,8,72]{6,3,5,2,4,1,0:T(8,128)(2,1)} %fusion.70) | copy-start | bytes 442372
  623.7 16.3 %all-to-all-start.9 = ((bf16[1,1,2,64,8]{4,2,1,0,3:T(2,128)(2,1)}), bf16[1,1,2,64,8]{4,2,1,0,3:T(2,128)(2,1)S(1)}, u32[]{:S(2)}, u32[]{:S(2)}) async-start(bf16[1,1,2,64,8]{4,2,1,0,3:T(2,128)(2,1)} %copy.465), calls=%async_computation.9 | async-start | bytes 65536 | tf_op jit(solution)/shard_map/all_to_all | solution.py:130
  631.2 17.9 %copy-start.21 = (f32[8,8,2]{1,0,2:T(8,128)S(1)}, f32[8,8,2]{1,0,2:T(8,128)}, u32[]{:S(2)}) copy-start(f32[8,8,2]{1,0,2:T(8,128)} %copy-done.20) | copy-start | bytes 1540
  634.9 33.9 %copy-start.3 = (bf16[1,1,64,2,1,8,72]{6,5,4,2,3,1,0:T(8,128)(2,1)S(1)}, bf16[1,1,64,2,1,8,72]{6,5,4,2,3,1,0:T(8,128)(2,1)}, u32[]{:S(2)}) copy-start(bf16[1,1,64,2,1,8,72]{6,5,4,2,3,1,0:T(8,128)(2,1)} %copy-done.2) | copy-start | bytes 442372
  634.9 33.9 %copy-start.29 = (f32[8]{0:T(128)S(1)}, f32[8]{0:T(128)}, u32[]{:S(2)}) copy-start(f32[8]{0:T(128)} %copy-done.28) | copy-start | bytes 100
  636.2 33.7 %copy-start.5 = (f32[2,8,64,64]{2,3,1,0:T(8,128)S(1)}, f32[2,8,64,64]{2,3,1,0:T(8,128)}, u32[]{:S(2)}) copy-start(f32[2,8,64,64]{2,3,1,0:T(8,128)} %copy-done.4) | copy-start | bytes 786436
  640.0 21.3 %all-to-all-start.7 = ((bf16[1,1,2,64,1152]{4,2,1,0,3:T(2,128)(2,1)}), bf16[1,1,2,64,1152]{4,2,1,0,3:T(2,128)(2,1)S(1)}, u32[]{:S(2)}, u32[]{:S(2)}) async-start(bf16[1,1,2,64,1152]{4,2,1,0,3:T(2,128)(2,1)} %copy.445), calls=%async_computation.7 | async-start | bytes 589824 | tf_op jit(solution)/shard_map/all_to_all | solution.py:129
  662.3 12.5 %copy-start.8 = (f32[1,1,64,2,8,72]{5,2,4,3,1,0:T(8,128)S(1)}, f32[1,1,64,2,8,72]{5,2,4,3,1,0:T(8,128)}, u32[]{:S(2)}) copy-start(f32[1,1,64,2,8,72]{5,2,4,3,1,0:T(8,128)} %get-tuple-element.44) | copy-start | bytes 884740
  676.9 19.4 %all-to-all-start.10 = ((bf16[8,2,128]{2,1,0:T(2,128)(2,1)}), bf16[8,2,128]{2,1,0:T(2,128)(2,1)S(1)}, u32[]{:S(2)}, u32[]{:S(2)}) async-start(bf16[8,2,128]{2,1,0:T(2,128)(2,1)} %reshape.755), calls=%async_computation.10 | async-start | bytes 8192 | tf_op jit(solution)/shard_map/all_to_all | solution.py:137
  694.0 19.7 %copy-start.27 = (f32[8]{0:T(128)S(1)}, f32[8]{0:T(128)}, u32[]{:S(2)}) copy-start(f32[8]{0:T(128)} %copy-done.26) | copy-start | bytes 100
  696.3 14.5 %all-to-all-start.8 = ((bf16[1,1,64,2,1152]{4,3,1,0,2:T(2,128)(2,1)}), bf16[1,1,64,2,1152]{4,3,1,0,2:T(2,128)(2,1)S(1)}, u32[]{:S(2)}, u32[]{:S(2)}) async-start(bf16[1,1,64,2,1152]{4,3,1,0,2:T(2,128)(2,1)} %copy.451), calls=%async_computation.8 | async-start | bytes 589824 | tf_op jit(solution)/shard_map/all_to_all | solution.py:136
  (20 other events, 97.4 us)
Sparse Core Ops, SparseCore 0:
  171.2 146.2 all-gather.6
  350.0 150.5 all-gather.8
  504.1 90.5 all-gather.10
